TPU v7x, 32 devices: a whole 2x2x4 slice. The times are simulated.
32 devices in a mesh: dp: 4 (over y, x), section: 2 (over core), tensor: 4 (over z).
Axes of the slice: x: 2, y: 2, z: 4, core: 2. Of those that a mesh axis runs over, the one named last changes fastest.
Arguments:
- stored: bfloat16 [2, 2, 256, 8192], P('section', None, 'dp', 'tensor'), may hold values from -6 to 6
- cotangent: bfloat16 [2, 32, 8192], P(None, None, 'tensor'), may hold values from -12 to 12
- positions: int32 [2, 32], replicated, may hold values from 128 to 255, as said below
- lengths: int32 [2], replicated, may hold values from 128 to 256, as said below
- norm_gain: float32 [2, 8192], P('section'), may hold values from 0.5 to 1.5
- w_query: bfloat16 [2, 8192, 8192], P('section', None, 'tensor')
- w_key: bfloat16 [2, 8192, 1024], P('section', None, 'tensor')
- w_value: bfloat16 [2, 8192, 1024], P('section', None, 'tensor'), may hold values from -0.0625 to 0.0625
- w_out: bfloat16 [2, 8192, 8192], P('section', 'tensor', 'dp'), may hold values from -0.0625 to 0.0625
Outputs:
- input_grads: float32 [2, 2, 256, 8192], P('section', None, 'dp', 'tensor')
Inputs may be any that keep to these rules, and one draw needn't show every extreme that they name: In each sequence the response positions are distinct, rise along the last dimension, lie in the last 128 positions, and the last one is 255. `lengths`: some sequence has length 256.
All inputs are finite; a program needn't handle non-finite values.
Results may differ from a plain program's by a relative error of at most 0.017.
Values may be sent and summed in bfloat16 or wider, within the bound.
A program may use at most 256 MiB of HBM per device.

v0:
```python
import math
import jax
import jax.numpy as jnp
from jax import lax
from jax.sharding import PartitionSpec as P

HD = 128
EPS = 1e-05
THETA = 500000.0


def passed_along(value, axis, steps):
    count = lax.axis_size(axis)
    leading, last = (max(0, -steps), min(count, count - steps))
    return lax.ppermute(value, axis, [(source, source + steps) for source in range(leading, last)])


def angle_tables(row_places):
    half_dim = HD // 2
    frequency = THETA ** (-(jnp.arange(half_dim, dtype=jnp.float32) * 2.0) / HD)
    angles = row_places[:, None] * frequency[None, :]
    cosine = jnp.concatenate([jnp.cos(angles), jnp.cos(angles)], -1)[:, None, :]
    sine_table = jnp.concatenate([jnp.sin(angles), jnp.sin(angles)], -1)[:, None, :]
    return (cosine, sine_table)


def turn_half(values):
    half_dim = values.shape[-1] // 2
    return jnp.concatenate([-values[..., half_dim:], values[..., :half_dim]], -1)


def rotate(values, cosine, sine_table):
    return values * cosine + turn_half(values) * sine_table


def unrotate(values, cosine, sine_table):
    return values * cosine - turn_half(values * sine_table)


def layer_grad(own_input, own_upstream, seq_lengths, gain, w_query, w_key, w_value, w_out):
    batch, rows, width_dev = own_input.shape
    kv_dev = w_key.shape[1] // HD
    q_dev = w_query.shape[1] // HD
    group = q_dev // kv_dev
    scale = 1.0 / math.sqrt(HD)
    x_whole, g_whole = (
        lax.all_gather(own_input, "tensor", axis=2, tiled=True),
        lax.all_gather(own_upstream, "tensor", axis=2, tiled=True),
    )
    width = x_whole.shape[2]
    x_full = x_whole.astype(jnp.float32)
    inv_rms = lax.rsqrt(jnp.mean(x_full * x_full, -1, keepdims=True) + EPS)
    normed = (x_full * inv_rms * gain).astype(jnp.bfloat16)
    first_row = lax.axis_index("dp") * rows
    query_ids = first_row + jnp.arange(rows, dtype=jnp.int32)
    cosine, sine_table = angle_tables(query_ids.astype(jnp.float32))
    queries = jnp.einsum(
        "bpd,dc->bpc", normed, w_query, preferred_element_type=jnp.float32
    ).reshape(batch, rows, q_dev, HD)
    keys = jnp.einsum("bpd,dc->bpc", normed, w_key, preferred_element_type=jnp.float32).reshape(
        batch, rows, kv_dev, HD
    )
    values = jnp.einsum("bpd,dc->bpc", normed, w_value, preferred_element_type=jnp.float32).reshape(
        batch, rows, kv_dev, HD
    )
    q_rot = rotate(queries, cosine, sine_table).astype(jnp.bfloat16)
    k_rot = rotate(keys, cosine, sine_table).astype(jnp.bfloat16)
    values_b = values.astype(jnp.bfloat16)
    grad_out = jnp.einsum("bpd,cd->bpc", g_whole, w_out, preferred_element_type=jnp.float32).astype(
        jnp.bfloat16
    )
    all_keys, all_values = (
        lax.all_gather(k_rot, "dp", axis=1, tiled=True),
        lax.all_gather(values_b, "dp", axis=1, tiled=True),
    )
    length = all_keys.shape[1]
    q_five = q_rot.reshape(batch, rows, kv_dev, group, HD)
    o_five = grad_out.reshape(batch, rows, kv_dev, group, HD)
    key_ids = jnp.arange(length, dtype=jnp.int32)
    causal = key_ids[None, None, :] <= query_ids[None, :, None]
    start_pos = length - seq_lengths
    inside = (key_ids[None, None, :] >= start_pos[:, None, None]) | (
        key_ids[None, None, :] == query_ids[None, :, None]
    )
    allowed = (causal & inside)[:, None, None, :, :]
    scores = (
        jnp.einsum("bpkgd,bjkd->bkgpj", q_five, all_keys, preferred_element_type=jnp.float32)
        * scale
    )
    masked = jnp.where(allowed, scores, -1e30)
    highest = jnp.max(masked, -1, keepdims=True)
    expo_terms = jnp.where(allowed, jnp.exp(masked - highest), 0.0)
    probs = expo_terms / jnp.sum(expo_terms, -1, keepdims=True)
    grad_probs = jnp.einsum(
        "bpkgd,bjkd->bkgpj", o_five, all_values, preferred_element_type=jnp.float32
    )
    row_dot = jnp.sum(probs * grad_probs, -1, keepdims=True)
    grad_scores = (probs * (grad_probs - row_dot) * scale).astype(jnp.bfloat16)
    probs_b = probs.astype(jnp.bfloat16)
    grad_qr = jnp.einsum(
        "bkgpj,bjkd->bpkgd", grad_scores, all_keys, preferred_element_type=jnp.float32
    )
    key_terms = jnp.einsum(
        "bkgpj,bpkgd->bjkd", grad_scores, q_five, preferred_element_type=jnp.float32
    )
    value_terms = jnp.einsum(
        "bkgpj,bpkgd->bjkd", probs_b, o_five, preferred_element_type=jnp.float32
    )
    grad_kr, grad_vr = (
        lax.psum_scatter(
            key_terms.astype(jnp.bfloat16), "dp", scatter_dimension=1, tiled=True
        ).astype(jnp.float32),
        lax.psum_scatter(
            value_terms.astype(jnp.bfloat16), "dp", scatter_dimension=1, tiled=True
        ).astype(jnp.float32),
    )
    grad_q = (
        unrotate(grad_qr.reshape(batch, rows, q_dev, HD), cosine, sine_table)
        .astype(jnp.bfloat16)
        .reshape(batch, rows, q_dev * HD)
    )
    grad_k = (
        unrotate(grad_kr, cosine, sine_table).astype(jnp.bfloat16).reshape(batch, rows, kv_dev * HD)
    )
    grad_v = grad_vr.astype(jnp.bfloat16).reshape(batch, rows, kv_dev * HD)
    partial_term = jnp.einsum("bpc,dc->bpd", grad_q, w_query, preferred_element_type=jnp.float32)
    partial_term = partial_term + jnp.einsum(
        "bpc,dc->bpd", grad_k, w_key, preferred_element_type=jnp.float32
    )
    partial_term = partial_term + jnp.einsum(
        "bpc,dc->bpd", grad_v, w_value, preferred_element_type=jnp.float32
    )
    summed = lax.psum(partial_term.astype(jnp.bfloat16), "tensor").astype(jnp.float32)
    stat = jnp.sum(x_full * gain * summed, -1, keepdims=True)
    whole_grad = (
        g_whole.astype(jnp.float32) + inv_rms * gain * summed - x_full * inv_rms**3 * stat / width
    )
    return lax.dynamic_slice_in_dim(whole_grad, lax.axis_index("tensor") * width_dev, width_dev, 2)


def on_device(stored, cotangent, positions, lengths, norm_gain, w_query, w_key, w_value, w_out):
    own_input = stored[0]
    gain = norm_gain[0]
    wq_layer = w_query[0]
    wk_layer = w_key[0]
    wv_layer = w_value[0]
    wo_layer = lax.all_gather(w_out[0], "dp", axis=1, tiled=True)
    seqs, rows, width_dev = own_input.shape
    section_id = lax.axis_index("section")
    row_ids = lax.axis_index("dp") * rows + jnp.arange(rows, dtype=jnp.int32)
    placed = (positions[:, None, :] == row_ids[None, :, None]).astype(jnp.bfloat16)
    from_loss = jnp.einsum(
        "spr,srd->spd", placed, cotangent, preferred_element_type=jnp.float32
    ).astype(jnp.bfloat16)

    def run_layer(input_part, upstream_part, length_part):
        return layer_grad(
            input_part, upstream_part, length_part, gain, wq_layer, wk_layer, wv_layer, wo_layer
        )

    first_in = jnp.where(section_id == 1, from_loss, jnp.zeros_like(from_loss))
    first_pass = run_layer(own_input, first_in, lengths)
    handed = passed_along(first_pass.astype(jnp.bfloat16), "section", -1)
    second_pass = run_layer(own_input, handed, lengths)
    result = jnp.where(section_id == 0, second_pass, first_pass)
    return result[None]


def solution(mesh):
    return jax.shard_map(
        on_device,
        mesh=mesh,
        in_specs=(
            P("section", None, "dp", "tensor"),
            P(None, None, "tensor"),
            P(),
            P(),
            P("section", None),
            P("section", None, "tensor"),
            P("section", None, "tensor"),
            P("section", None, "tensor"),
            P("section", "tensor", "dp"),
        ),
        out_specs=P("section", None, "dp", "tensor"),
        check_vma=False,
    )
```

profile of v0, /device:TPU:0, one launch (start us, length us, event | category | flops | bytes accessed | tf_op | source)
XLA Modules:
  0.0 914.5 jit_solution(1680415631563956756)
XLA Ops:
  6.5 0.7 all-gather.11.cloned.1.call-update
  7.5 2.0 fusion.50
  9.5 0.7 all-gather.13.cloned.1.call-update
  10.3 40.0 %copy.63 = bf16[2048,8192]{1,0:T(8,128)(2,1)} copy(bf16[2048,8192]{0,1:T(8,128)(2,1)} %bitcast.235) | data formatting | bytes 67108864 | tf_op jit(solution)/shard_map/bpd,dc->bpc/dot_general | solution.py:57
  50.3 6.4 copy.62
  56.7 6.4 copy.64
  63.1 0.6 dynamic-slice
  64.9 2.3 fusion.33
  67.4 3.9 fusion.117
  71.5 10.4 %all_gather.23 = bf16[2,256,2,128]{3,1,2,0:T(8,128)(2,1)S(1)} all-gather(bf16[2,64,2,128]{3,1,2,0:T(8,128)(2,1)S(1)} %fusion.113), channel_id=1, replica_groups=mesh['dp'=4,'section'=2,'tensor'=4] {'dp'}, dimensions={1}, use_global_device_ids=true | all-gather | bytes 327680 | tf_op jit(solution)/shard_map/all_gather | solution.py:73
  81.9 1.5 convolution_convert_fusion.1
  83.4 9.6 %all_gather.24 = bf16[2,256,2,128]{3,1,2,0:T(8,128)(2,1)S(1)} all-gather(bf16[2,64,2,128]{3,1,2,0:T(8,128)(2,1)S(1)} %convolution_convert_fusion.1), channel_id=1, replica_groups=mesh['dp'=4,'section'=2,'tensor'=4] {'dp'}, dimensions={1}, use_global_device_ids=true | all-gather | bytes 327680 | tf_op jit(solution)/shard_map/all_gather | solution.py:74
  93.1 15.8 %fusion.115 = f32[2,64,16,128]{3,1,2,0:T(8,128)S(1)} fusion(bf16[16,128,8192,1]{2,1,0,3:T(8,128)(2,1)} %bitcast.236, bf16[1,2,64,8192]{3,2,1,0:T(8,128)(2,1)S(1)} %copy-done.2, f32[8192]{0:T(1024)S(1)} %bitcast.253, f32[2,64]{1,0:T(2,128)S(1)} %get-tuple-element.23), kind=kOutput, calls=%fused_computation.131 | convolution fusion | flops 4299161600 | bytes 36733440 | tf_op jit(solution)/shard_map/bpd,dc->bpc/dot_general | solution.py:57
  108.9 0.4 slice_negate_fusion.2
  109.3 0.4 fusion.74
  109.7 2.3 fusion.146
  112.0 3.8 fusion.143
  115.8 285.4 %all-gather.13.cloned.1.call-done = bf16[1,2048,8192]{2,1,0:T(8,128)(2,1)} async-done(((bf16[1,2048,2048]{2,1,0:T(8,128)(2,1)}), bf16[1,2048,8192]{2,1,0:T(8,128)(2,1)}) %all-gather.13.cloned.1.call-update) | async-done | bytes 33554448 | tf_op jit(solution)/shard_map/all_gather | solution.py:147
  401.2 16.4 %fusion.44 = bf16[2,64,2048]{2,1,0:T(8,128)(2,1)S(1)} fusion(bf16[2,64,8192]{2,1,0:T(8,128)(2,1)} %all-gather.7.cloned.1.call-done, bf16[1,2048,8192]{2,1,0:T(8,128)(2,1)} %all-gather.13.cloned.1.call-done), kind=kOutput, calls=%fused_computation.36 | convolution fusion | flops 4295229440 | bytes 36175872 | tf_op jit(solution)/shard_map/bpd,cd->bpc/dot_general | solution.py:69
  417.7 0.8 copy-done.13
  418.5 1.7 fusion.96
  420.2 15.5 %fusion.77 = f32[2,2,128,8,64]{2,4,3,1,0:T(8,128)} fusion(f32[2,2,256,64,8]{2,3,4,1,0:T(8,128)} %fusion.96, bf16[2,256,2,128]{3,1,2,0:T(8,128)(2,1)S(1)} %all_gather.23, f32[2,2,8,64,256]{4,3,2,1,0:T(8,128)} %get-tuple-element.29, f32[2,2,8,64]{3,2,1,0:T(8,128)S(1)} %get-tuple-element.28), kind=kOutput, calls=%fused_computation.86 | convolution fusion | flops 137890048 | bytes 5513216 | tf_op jit(solution)/shard_map/bkgpj,bjkd->bpkgd/dot_general | solution.py:100
  435.7 1.4 broadcast_multiply_fusion.2
  437.2 0.3 copy-done.15
  437.4 1.5 fusion.65
  438.9 1.8 copy.45
  440.7 0.6 reduce-scatter.3.cloned.1.call-start
  441.3 1.7 slice_negate_fusion.1
  443.0 16.3 %fusion.66 = bf16[2,256,2,128]{3,1,2,0:T(8,128)(2,1)} fusion(bf16[2,64,2,8,128]{4,1,3,2,0:T(8,128)(2,1)} %bitcast.257, f32[2,2,256,64,8]{2,3,4,1,0:T(8,128)} %fusion.96, f32[2,2,8,64,256]{4,3,2,1,0:T(8,128)} %get-tuple-element.29, f32[2,2,8,64]{3,2,1,0:T(8,128)S(1)} %get-tuple-element.28), kind=kOutput, calls=%fused_computation.66 | convolution fusion | flops 138021120 | bytes 4988928 | tf_op jit(solution)/shard_map/bkgpj,bpkgd->bjkd/dot_general | solution.py:103
  459.4 24.7 %all-reduce.11.cloned.1.call-done = bf16[2,256,2,128]{3,2,0,1:T(2,128)(2,1)} async-done(((bf16[2,256,2,128]{3,2,0,1:T(2,128)(2,1)}), bf16[2,256,2,128]{3,2,0,1:T(2,128)(2,1)}) %all-reduce.11.cloned.1.call-update) | async-done | bytes 262160
  484.1 0.9 constant_dynamic-slice_fusion.1
  485.0 5.8 fusion.38
  490.8 20.3 %reduce-scatter.3.cloned.1.call-done = bf16[2,64,2,128]{3,1,2,0:T(8,128)(2,1)} async-done(((bf16[2,256,2,128]{3,1,2,0:T(8,128)(2,1)}), bf16[2,64,2,128]{3,1,2,0:T(8,128)(2,1)}) %reduce-scatter.3.cloned.1.call-update) | async-done | bytes 65552 | tf_op jit(solution)/shard_map/reduce_scatter | solution.py:110
  511.1 0.9 convert_multiply_fusion.6
  512.0 5.8 fusion.42
  517.8 19.2 %fusion.26 = bf16[2,64,8192]{2,1,0:T(8,128)(2,1)} fusion(f32[2,64,8192]{2,1,0:T(8,128)} %fusion.38, f32[2,64,8192]{2,1,0:T(8,128)} %fusion.42, bf16[1,8192,2048]{2,1,0:T(8,128)(2,1)} %param.14, f32[2,64,16,64]{3,1,2,0:T(8,128)} %get-tuple-element.12, f32[2,64,16,64]{3,1,2,0:T(8,128)} %get-tuple-element.11, f32[2,64,16,128]{3,1,2,0:T(8,128)S(1)} %bitcast.242, ...), kind=kOutput, calls=%fused_computation.16 | convolution fusion | flops 4299161600 | bytes 46170112 | tf_op jit(solution)/shard_map/bpc,dc->bpd/dot_general | solution.py:126
  537.1 86.2 %all-reduce.7.cloned.1.call-done = bf16[2,64,8192]{2,1,0:T(8,128)(2,1)} async-done(((bf16[2,64,8192]{2,1,0:T(8,128)(2,1)}), bf16[2,64,8192]{2,1,0:T(8,128)(2,1)}) %all-reduce.7.cloned.1.call-update) | async-done | bytes 2097168 | tf_op jit(solution)/shard_map/psum | solution.py:133
  623.4 2.2 convert_element_type.155
  625.6 2.0 convert_multiply_fusion.1
  627.6 3.4 fusion.144
  631.1 1.3 collective-permute-start
  632.4 2.5 collective-permute-done
  634.9 0.8 copy-done.19
  636.0 44.6 %all-gather.9.cloned.1.call-done = bf16[2,64,8192]{2,1,0:T(8,128)(2,1)} async-done(((bf16[2,64,2048]{2,1,0:T(8,128)(2,1)}), bf16[2,64,8192]{2,1,0:T(8,128)(2,1)}) %all-gather.9.cloned.1.call-update) | async-done | bytes 2097168 | tf_op jit(solution)/shard_map/all_gather | solution.py:48
  680.6 16.4 %fusion.47 = bf16[2,64,2048]{2,1,0:T(8,128)(2,1)S(1)} fusion(bf16[2,64,8192]{2,1,0:T(8,128)(2,1)} %all-gather.9.cloned.1.call-done, bf16[1,2048,8192]{2,1,0:T(8,128)(2,1)} %all-gather.13.cloned.1.call-done), kind=kOutput, calls=%fused_computation.37 | convolution fusion | flops 4295229440 | bytes 36175872 | tf_op jit(solution)/shard_map/bpd,cd->bpc/dot_general | solution.py:69
  697.1 1.8 fusion.93
  698.9 1.5 fusion.63
  700.4 15.6 %fusion.79 = f32[2,2,128,8,64]{2,4,3,1,0:T(8,128)} fusion(f32[2,2,256,64,8]{2,3,4,1,0:T(8,128)} %fusion.93, bf16[2,256,2,128]{3,1,2,0:T(8,128)(2,1)S(1)} %copy-done.21, f32[2,2,8,64,256]{4,3,2,1,0:T(8,128)} %get-tuple-element.29, f32[2,2,8,64]{3,2,1,0:T(8,128)S(1)} %get-tuple-element.28), kind=kOutput, calls=%fused_computation.88 | convolution fusion | flops 137890048 | bytes 5513216 | tf_op jit(solution)/shard_map/bkgpj,bjkd->bpkgd/dot_general | solution.py:100
  716.0 1.3 broadcast_multiply_fusion.1
  717.3 1.8 copy.53
  719.2 1.8 slice_negate_fusion
  721.0 16.3 %fusion.64 = bf16[2,256,2,128]{3,1,2,0:T(8,128)(2,1)} fusion(bf16[2,64,2,8,128]{4,1,3,2,0:T(8,128)(2,1)} %bitcast.258, f32[2,2,256,64,8]{2,3,4,1,0:T(8,128)} %fusion.93, f32[2,2,8,64,256]{4,3,2,1,0:T(8,128)} %get-tuple-element.29, f32[2,2,8,64]{3,2,1,0:T(8,128)S(1)} %get-tuple-element.28), kind=kOutput, calls=%fused_computation.64 | convolution fusion | flops 138021120 | bytes 4988928 | tf_op jit(solution)/shard_map/bkgpj,bpkgd->bjkd/dot_general | solution.py:103
  737.6 23.7 %all-reduce.13.cloned.1.call-done = bf16[2,256,2,128]{3,2,0,1:T(2,128)(2,1)} async-done(((bf16[2,256,2,128]{3,2,0,1:T(2,128)(2,1)}), bf16[2,256,2,128]{3,2,0,1:T(2,128)(2,1)}) %all-reduce.13.cloned.1.call-update) | async-done | bytes 262160
  761.3 0.9 constant_dynamic-slice_fusion
  762.2 5.6 fusion.36
  767.9 20.6 %reduce-scatter.5.cloned.1.call-done = bf16[2,64,2,128]{3,1,2,0:T(8,128)(2,1)} async-done(((bf16[2,256,2,128]{3,1,2,0:T(8,128)(2,1)}), bf16[2,64,2,128]{3,1,2,0:T(8,128)(2,1)}) %reduce-scatter.5.cloned.1.call-update) | async-done | bytes 65552 | tf_op jit(solution)/shard_map/reduce_scatter | solution.py:110
  788.4 0.9 convert_multiply_fusion.4
  789.4 5.8 fusion.40
  795.2 19.3 %fusion.23 = bf16[2,64,8192]{2,1,0:T(8,128)(2,1)} fusion(f32[2,64,8192]{2,1,0:T(8,128)} %fusion.36, f32[2,64,8192]{2,1,0:T(8,128)} %fusion.40, bf16[1,8192,2048]{2,1,0:T(8,128)(2,1)} %param.14, f32[2,64,16,64]{3,1,2,0:T(8,128)} %get-tuple-element.10, f32[2,64,16,64]{3,1,2,0:T(8,128)} %get-tuple-element.9, f32[2,64,16,128]{3,1,2,0:T(8,128)S(1)} %bitcast.240, ...), kind=kOutput, calls=%fused_computation.15 | convolution fusion | flops 4299161600 | bytes 46170112 | tf_op jit(solution)/shard_map/bpc,dc->bpd/dot_general | solution.py:126
  814.6 86.3 %all-reduce.9.cloned.1.call-done = bf16[2,64,8192]{2,1,0:T(8,128)(2,1)} async-done(((bf16[2,64,8192]{2,1,0:T(8,128)(2,1)}), bf16[2,64,8192]{2,1,0:T(8,128)(2,1)}) %all-reduce.9.cloned.1.call-update) | async-done | bytes 2097168 | tf_op jit(solution)/shard_map/psum | solution.py:133
  900.8 2.2 convert_element_type.169
  903.1 0.9 fusion.32
  904.0 0.3 copy-done.10
  904.3 3.1 fusion.70
  (81 shorter events, 2.7 us)
Async XLA Ops:
  6.5 1.0 copy-start
  6.5 58.4 %all-gather.11.cloned.1.call-start = ((), (), s32[]{:S(2)}) async-start(), calls=%async_computation.8 | async-start | bytes 2621440 | tf_op jit(solution)/shard_map/all_gather | solution.py:47
  7.3 108.6 %all-gather.7.cloned.1.call-start = ((), (), s32[]{:S(2)}) async-start(), calls=%async_computation.2 | async-start | bytes 2621440 | tf_op jit(solution)/shard_map/all_gather | solution.py:48
  9.5 391.7 %all-gather.13.cloned.1.call-start = ((), (), s32[]{:S(2)}) async-start(), calls=%async_computation.9 | async-start | bytes 41943040 | tf_op jit(solution)/shard_map/all_gather | solution.py:147
  10.2 473.9 %all-reduce.11.cloned.1.call-start = ((), (), s32[]{:S(2)}) async-start(), calls=%async_computation.10 | async-start | bytes 524288
  56.7 6.4 copy-start.23
  56.7 8.0 copy-start.22
  63.1 4.2 copy-start.17
  64.9 2.4 copy-start.2
  67.4 14.5 %copy-start.9 = (bf16[256,8192]{1,0:T(8,128)(2,1)S(1)}, bf16[256,8192]{1,0:T(8,128)(2,1)}, u32[]{:S(2)}) copy-start(bf16[256,8192]{1,0:T(8,128)(2,1)} %copy.64) | copy-start | bytes 12582916
  81.9 338.3 %copy-start.20 = (bf16[2,256,2,128]{3,1,2,0:T(8,128)(2,1)}, bf16[2,256,2,128]{3,1,2,0:T(8,128)(2,1)S(1)}, u32[]{:S(2)}) copy-start(bf16[2,256,2,128]{3,1,2,0:T(8,128)(2,1)S(1)} %all_gather.23) | copy-start | bytes 786436
  93.1 324.6 %copy-start.11 = (bf16[2,256,2,128]{3,1,2,0:T(8,128)(2,1)}, bf16[2,256,2,128]{3,1,2,0:T(8,128)(2,1)S(1)}, u32[]{:S(2)}) copy-start(bf16[2,256,2,128]{3,1,2,0:T(8,128)(2,1)S(1)} %all_gather.24) | copy-start | bytes 786436
  109.7 2.3 copy-start.18
  417.7 0.8 copy-start.13
  435.7 1.4 copy-start.14
  435.7 1.7 copy-start.15
  440.7 70.3 %reduce-scatter.3.cloned.1.call-start = ((), (), s32[]{:S(2)}) async-start(), calls=%async_computation.3 | async-start | bytes 327680 | tf_op jit(solution)/shard_map/reduce_scatter | solution.py:110
  459.3 164.0 %all-reduce.7.cloned.1.call-start = ((), (), s32[]{:S(2)}) async-start(), calls=%async_computation.4 | async-start | bytes 4194304 | tf_op jit(solution)/shard_map/psum | solution.py:133
  512.0 5.8 copy-start.8
  537.1 143.5 %all-gather.9.cloned.1.call-start = ((), (), s32[]{:S(2)}) async-start(), calls=%async_computation.5 | async-start | bytes 2621440 | tf_op jit(solution)/shard_map/all_gather | solution.py:48
  623.4 2.2 copy-start.6
  627.5 3.4 copy-start.3
  627.5 3.6 copy-start.4
  631.1 3.8 collective-permute-start
  634.9 0.8 copy-start.19
  635.7 61.4 %copy-start.12 = (bf16[2,256,2,128]{3,1,2,0:T(8,128)(2,1)S(1)}, bf16[2,256,2,128]{3,1,2,0:T(8,128)(2,1)}, u32[]{:S(2)}) copy-start(bf16[2,256,2,128]{3,1,2,0:T(8,128)(2,1)} %copy-done.11) | copy-start | bytes 786436
  635.8 125.5 %all-reduce.13.cloned.1.call-start = ((), (), s32[]{:S(2)}) async-start(), calls=%async_computation.11 | async-start | bytes 524288
  697.0 1.9 copy-start.16
  697.1 3.3 copy-start.21
  719.1 69.3 %reduce-scatter.5.cloned.1.call-start = ((), (), s32[]{:S(2)}) async-start(), calls=%async_computation.6 | async-start | bytes 327680 | tf_op jit(solution)/shard_map/reduce_scatter | solution.py:110
  737.3 163.5 %all-reduce.9.cloned.1.call-start = ((), (), s32[]{:S(2)}) async-start(), calls=%async_computation.7 | async-start | bytes 4194304 | tf_op jit(solution)/shard_map/psum | solution.py:133
  789.4 5.8 copy-start.7
  900.8 2.2 copy-start.5
  903.1 1.2 copy-start.10
  904.0 3.4 copy-start.1
Sparse Core Ops, SparseCore 0:
  8.9 48.3 all-gather.10
  58.9 44.4 all-gather.6
  105.3 295.8 all-gather.12
  440.9 43.1 all-reduce.10
  486.7 24.3 reduce-scatter.2
  537.2 86.1 all-reduce.6
  635.9 44.6 all-gather.8
  719.3 41.9 all-reduce.12
  764.1 24.3 reduce-scatter.4
  814.7 86.1 all-reduce.8
where the time goes:
time: 921 us; the launch traced here: 914 us
  waiting for transfers between devices  596 us (65%)
  matrix products  190 us (21%)
  local copies, waits for them, and re-layouts  62 us (7%)
  other arithmetic  29.4 us (3%)
  blocking collectives  20 us (2%)
  between operations  14.8 us (2%)
    all_gather x1, waiting for transfers between devices, on_device(): wo_layer = lax.all_gather(w_out[0], 'dp', axis=1, tiled=True)  285 us
    psum x2, waiting for transfers between devices, layer_grad(): lax.psum(partial_term.astype(jnp.bfloat16), 'tensor').astype(jnp.float32)  172 us
    unnamed x12, waiting for transfers between devices  49.9 us
    all_gather x2, waiting for transfers between devices, layer_grad(): lax.all_gather(own_upstream, 'tensor', axis=2, tiled=True)  44.6 us
    reduce_scatter x2, waiting for transfers between devices, layer_grad(): lax.psum_scatter(key_terms.astype(jnp.bfloat16), 'dp', scatter_dimension=...  40.8 us
    dot_general x1, local copies, waits for them, and re-layouts, layer_grad(): jnp.einsum('bpd,dc->bpc', normed, w_query, preferred_element_type=jnp.flo...  40 us
    dot_general x2, matrix products, layer_grad(): jnp.einsum('bpc,dc->bpd', grad_q, w_query, preferred_element_type=jnp.flo...  38.6 us
    dot_general x2, matrix products, layer_grad(): jnp.einsum('bpd,cd->bpc', g_whole, w_out, preferred_element_type=jnp.floa...  32.7 us
  transfers between devices with their start and end apart: 11, of which 9 were waited for; matrix products, arithmetic and copies ran while one was open for 15% of the time, Pallas kernels for 0%

commit v1 on v0

--- a/solution.py
+++ b/solution.py
@@ -7,6 +7,17 @@
 HD = 128
 EPS = 1e-05
 THETA = 500000.0
+
+
+def collect(x, axis, dim):
+    ways = lax.axis_size(axis)
+    pieces = [x]
+    for far in range(1, ways):
+        pieces.append(
+            lax.ppermute(pieces[far - 1], axis, [(d, (d - 1) % ways) for d in range(ways)])
+        )
+    line = jnp.concatenate(pieces, axis=dim)
+    return jnp.roll(line, lax.axis_index(axis) * x.shape[dim], axis=dim)
 
 
 def passed_along(value, axis, steps):
@@ -45,7 +56,7 @@
     scale = 1.0 / math.sqrt(HD)
     x_whole, g_whole = (
         lax.all_gather(own_input, "tensor", axis=2, tiled=True),
-        lax.all_gather(own_upstream, "tensor", axis=2, tiled=True),
+        collect(own_upstream, "tensor", 2),
     )
     width = x_whole.shape[2]
     x_full = x_whole.astype(jnp.float32)

time: 921 us -> 849 us (0.922)
  waiting for transfers between devices: 596 us -> 507 us
  starting transfers between devices: 2.56 us -> 19.4 us
    all_gather x1, waiting for transfers between devices: 285 us -> 211 us  [on_device(): wo_layer = lax.all_gather(w_out[0], 'dp', axis=1, tiled=True)]
    ppermute x0 -> x6, waiting for transfers between devices: none -> 55.4 us  [collect(): lax.ppermute(pieces[far - 1], axis, [(d, (d - 1) % ways) for d in range(w...]
    all_gather x2 -> x0, waiting for transfers between devices: 44.6 us -> none  [layer_grad(): lax.all_gather(own_upstream, 'tensor', axis=2, tiled=True)]
    unnamed x12 -> x10, waiting for transfers between devices: 49.9 us -> 24.6 us
    ppermute x0 -> x6, starting transfers between devices: none -> 17.4 us  [collect(): lax.ppermute(pieces[far - 1], axis, [(d, (d - 1) % ways) for d in range(w...]
  transfers between devices with their start and end apart: 11 -> 15, of which waited for: 9 -> 13; matrix products, arithmetic and copies ran while one was open for 15% -> 20% of each run, Pallas kernels for 0% -> 0%
where the time goes in v1:
time: 849 us; the launch traced here: 842 us
  waiting for transfers between devices  507 us (60%)
  matrix products  184 us (22%)
  local copies, waits for them, and re-layouts  58.2 us (7%)
  other arithmetic  34 us (4%)
  blocking collectives  24 us (3%)
  starting transfers between devices  19.4 us (2%)
  between operations  14.9 us (2%)
    all_gather x1, waiting for transfers between devices, on_device(): wo_layer = lax.all_gather(w_out[0], 'dp', axis=1, tiled=True)  211 us
    psum x2, waiting for transfers between devices, layer_grad(): lax.psum(partial_term.astype(jnp.bfloat16), 'tensor').astype(jnp.float32)  173 us
    ppermute x6, waiting for transfers between devices, collect(): lax.ppermute(pieces[far - 1], axis, [(d, (d - 1) % ways) for d in range(w...  55.4 us
    reduce_scatter x2, waiting for transfers between devices, layer_grad(): lax.psum_scatter(key_terms.astype(jnp.bfloat16), 'dp', scatter_dimension=...  40.8 us
    dot_general x1, local copies, waits for them, and re-layouts, layer_grad(): jnp.einsum('bpd,dc->bpc', normed, w_query, preferred_element_type=jnp.flo...  40.8 us
    dot_general x2, matrix products, layer_grad(): jnp.einsum('bpc,dc->bpd', grad_q, w_query, preferred_element_type=jnp.flo...  38.5 us
    dot_general x2, matrix products, layer_grad(): jnp.einsum('bpd,cd->bpc', g_whole, w_out, preferred_element_type=jnp.floa...  33.1 us
    dot_general x2, matrix products, layer_grad(): jnp.einsum('bkgpj,bpkgd->bjkd', grad_scores, q_five, preferred_element_ty...  32.7 us
  transfers between devices with their start and end apart: 15, of which 13 were waited for; matrix products, arithmetic and copies ran while one was open for 20% of the time, Pallas kernels for 0%

profile of v1, /device:TPU:0, one launch (start us, length us, event | category | flops | bytes accessed | tf_op | source)
XLA Modules:
  0.0 841.7 jit_solution(9857649494877500619)
XLA Ops:
  6.5 0.7 all-gather.5.cloned.1.call-update
  7.3 0.7 all-gather.7.cloned.1.call-update
  8.5 5.1 collective-permute-start
  13.7 40.8 %copy.63 = bf16[2048,8192]{1,0:T(8,128)(2,1)} copy(bf16[2048,8192]{0,1:T(8,128)(2,1)} %bitcast.235) | data formatting | bytes 67108864 | tf_op jit(solution)/shard_map/bpd,dc->bpc/dot_general | solution.py:68
  54.4 6.4 copy.62
  60.9 6.4 copy.64
  69.3 12.6 %collective-permute-done.1 = bf16[2,64,2048]{2,1,0:T(8,128)(2,1)S(1)} collective-permute-done((bf16[2,64,2048]{2,1,0:T(8,128)(2,1)S(1)}, bf16[2,64,2048]{2,1,0:T(8,128)(2,1)S(1)}, u32[]{:S(2)}, u32[]{:S(2)}) %collective-permute-start.1) | collective-permute-done | bytes 524320 | tf_op jit(solution)/shard_map/ppermute | solution.py:17
  81.9 2.2 collective-permute-start.2
  84.4 10.0 %collective-permute-done.2 = bf16[2,64,2048]{2,1,0:T(8,128)(2,1)S(1)} collective-permute-done((bf16[2,64,2048]{2,1,0:T(8,128)(2,1)S(1)}, bf16[2,64,2048]{2,1,0:T(8,128)(2,1)S(1)}, u32[]{:S(2)}, u32[]{:S(2)}) %collective-permute-start.2) | collective-permute-done | bytes 524320 | tf_op jit(solution)/shard_map/ppermute | solution.py:17
  94.4 4.6 fusion.61
  99.0 2.1 fusion.33
  101.2 4.5 fusion.131
  105.9 11.7 %all_gather.16 = bf16[2,256,2,128]{3,1,2,0:T(8,128)(2,1)S(1)} all-gather(bf16[2,64,2,128]{3,1,2,0:T(8,128)(2,1)S(1)} %fusion.127), channel_id=1, replica_groups=mesh['dp'=4,'section'=2,'tensor'=4] {'dp'}, dimensions={1}, use_global_device_ids=true | all-gather | bytes 327680 | tf_op jit(solution)/shard_map/all_gather | solution.py:84
  117.6 1.5 convolution_convert_fusion.1
  119.2 12.2 %all_gather.17 = bf16[2,256,2,128]{3,1,2,0:T(8,128)(2,1)S(1)} all-gather(bf16[2,64,2,128]{3,1,2,0:T(8,128)(2,1)S(1)} %convolution_convert_fusion.1), channel_id=1, replica_groups=mesh['dp'=4,'section'=2,'tensor'=4] {'dp'}, dimensions={1}, use_global_device_ids=true | all-gather | bytes 327680 | tf_op jit(solution)/shard_map/all_gather | solution.py:85
  131.4 15.8 %fusion.129 = f32[2,64,16,128]{3,1,2,0:T(8,128)S(1)} fusion(bf16[16,128,8192,1]{2,1,0,3:T(8,128)(2,1)} %bitcast.236, bf16[1,2,64,8192]{3,2,1,0:T(8,128)(2,1)S(1)} %copy-done.2, f32[8192]{0:T(1024)S(1)} %bitcast.253, f32[2,64]{1,0:T(2,128)S(1)} %get-tuple-element.24), kind=kOutput, calls=%fused_computation.161 | convolution fusion | flops 4299161600 | bytes 36733440 | tf_op jit(solution)/shard_map/bpd,dc->bpc/dot_general | solution.py:68
  148.0 2.2 fusion.160
  150.3 2.9 fusion.157
  153.2 211.2 %all-gather.7.cloned.1.call-done = bf16[1,2048,8192]{2,1,0:T(8,128)(2,1)} async-done(((bf16[1,2048,2048]{2,1,0:T(8,128)(2,1)}), bf16[1,2048,8192]{2,1,0:T(8,128)(2,1)}) %all-gather.7.cloned.1.call-update) | async-done | bytes 33554448 | tf_op jit(solution)/shard_map/all_gather | solution.py:158
  364.4 16.4 %fusion.44 = bf16[2,64,2048]{2,1,0:T(8,128)(2,1)S(1)} fusion(bf16[2,64,8192]{2,1,0:T(8,128)(2,1)} %fusion.61, bf16[1,2048,8192]{2,1,0:T(8,128)(2,1)} %all-gather.7.cloned.1.call-done), kind=kOutput, calls=%fused_computation.52 | convolution fusion | flops 4295229440 | bytes 36175872 | tf_op jit(solution)/shard_map/bpd,cd->bpc/dot_general | solution.py:80
  381.0 0.8 fusion.79
  381.8 0.9 copy.45
  382.7 1.7 fusion.110
  384.5 13.1 %fusion.91 = f32[2,2,128,8,64]{2,4,3,1,0:T(8,128)S(1)} fusion(f32[2,2,256,64,8]{2,3,4,1,0:T(8,128)} %fusion.110, bf16[2,256,2,128]{3,1,2,0:T(8,128)(2,1)} %copy-done.15, f32[2,2,8,64,256]{4,3,2,1,0:T(8,128)} %get-tuple-element.30, f32[2,2,8,64]{3,2,1,0:T(8,128)S(1)} %get-tuple-element.29), kind=kOutput, calls=%fused_computation.116 | convolution fusion | flops 137890048 | bytes 5513216 | tf_op jit(solution)/shard_map/bkgpj,bjkd->bpkgd/dot_general | solution.py:111
  397.7 1.7 slice_negate_fusion.1
  399.5 16.3 %fusion.80 = bf16[2,256,2,128]{3,1,2,0:T(8,128)(2,1)} fusion(bf16[2,64,2,8,128]{4,1,3,2,0:T(8,128)(2,1)} %bitcast.257, f32[2,2,256,64,8]{2,3,4,1,0:T(8,128)} %fusion.110, f32[2,2,8,64,256]{4,3,2,1,0:T(8,128)} %get-tuple-element.30, f32[2,2,8,64]{3,2,1,0:T(8,128)S(1)} %get-tuple-element.29), kind=kOutput, calls=%fused_computation.96 | convolution fusion | flops 138021120 | bytes 4988928 | tf_op jit(solution)/shard_map/bkgpj,bpkgd->bjkd/dot_general | solution.py:114
  416.0 10.0 %all-reduce.11.cloned.1.call-done = bf16[2,256,2,128]{3,2,0,1:T(2,128)(2,1)} async-done(((bf16[2,256,2,128]{3,2,0,1:T(2,128)(2,1)}), bf16[2,256,2,128]{3,2,0,1:T(2,128)(2,1)}) %all-reduce.11.cloned.1.call-update) | async-done | bytes 262160
  426.1 0.9 constant_dynamic-slice_fusion.1
  427.0 5.8 fusion.38
  432.8 20.3 %reduce-scatter.3.cloned.1.call-done = bf16[2,64,2,128]{3,1,2,0:T(8,128)(2,1)} async-done(((bf16[2,256,2,128]{3,1,2,0:T(8,128)(2,1)}), bf16[2,64,2,128]{3,1,2,0:T(8,128)(2,1)}) %reduce-scatter.3.cloned.1.call-update) | async-done | bytes 65552 | tf_op jit(solution)/shard_map/reduce_scatter | solution.py:121
  453.0 0.9 convert_multiply_fusion.6
  454.0 5.7 fusion.42
  459.7 19.2 %fusion.26 = bf16[2,64,8192]{2,1,0:T(8,128)(2,1)} fusion(f32[2,64,8192]{2,1,0:T(8,128)} %fusion.38, f32[2,64,8192]{2,1,0:T(8,128)} %fusion.42, bf16[1,8192,2048]{2,1,0:T(8,128)(2,1)} %param.16, f32[2,64,16,64]{3,1,2,0:T(8,128)} %get-tuple-element.13, f32[2,64,16,64]{3,1,2,0:T(8,128)} %get-tuple-element.12, f32[2,64,16,128]{3,1,2,0:T(8,128)S(1)} %bitcast.242, ...), kind=kOutput, calls=%fused_computation.16 | convolution fusion | flops 4299161600 | bytes 46170112 | tf_op jit(solution)/shard_map/bpc,dc->bpd/dot_general | solution.py:137
  479.0 86.2 %all-reduce.7.cloned.1.call-done = bf16[2,64,8192]{2,1,0:T(8,128)(2,1)} async-done(((bf16[2,64,8192]{2,1,0:T(8,128)(2,1)}), bf16[2,64,8192]{2,1,0:T(8,128)(2,1)}) %all-reduce.7.cloned.1.call-update) | async-done | bytes 2097168 | tf_op jit(solution)/shard_map/psum | solution.py:144
  565.2 2.2 convert_element_type.155
  567.5 1.9 convert_multiply_fusion.1
  569.4 3.4 fusion.158
  572.8 1.3 collective-permute-start.3
  574.1 2.5 collective-permute-done.3
  576.6 1.6 collective-permute-start.4
  578.2 12.3 %collective-permute-done.4 = bf16[2,64,2048]{2,1,0:T(8,128)(2,1)S(1)} collective-permute-done((bf16[2,64,2048]{2,1,0:T(8,128)(2,1)S(1)}, bf16[2,64,2048]{2,1,0:T(8,128)(2,1)S(1)}, u32[]{:S(2)}, u32[]{:S(2)}) %collective-permute-start.4) | collective-permute-done | bytes 524320 | tf_op jit(solution)/shard_map/ppermute | solution.py:17
  590.6 3.4 collective-permute-start.5
  594.0 10.6 %collective-permute-done.5 = bf16[2,64,2048]{2,1,0:T(8,128)(2,1)S(1)} collective-permute-done((bf16[2,64,2048]{2,1,0:T(8,128)(2,1)S(1)}, bf16[2,64,2048]{2,1,0:T(8,128)(2,1)S(1)}, u32[]{:S(2)}, u32[]{:S(2)}) %collective-permute-start.5) | collective-permute-done | bytes 524320 | tf_op jit(solution)/shard_map/ppermute | solution.py:17
  604.6 4.5 collective-permute-start.6
  609.1 9.8 %collective-permute-done.6 = bf16[2,64,2048]{2,1,0:T(8,128)(2,1)S(1)} collective-permute-done((bf16[2,64,2048]{2,1,0:T(8,128)(2,1)S(1)}, bf16[2,64,2048]{2,1,0:T(8,128)(2,1)S(1)}, u32[]{:S(2)}, u32[]{:S(2)}) %collective-permute-start.6) | collective-permute-done | bytes 524320 | tf_op jit(solution)/shard_map/ppermute | solution.py:17
  618.8 3.7 fusion.54
  622.6 16.7 %fusion.47 = bf16[2,64,2048]{2,1,0:T(8,128)(2,1)S(1)} fusion(bf16[2,64,8192]{2,1,0:T(8,128)(2,1)S(1)} %fusion.54, bf16[1,2048,8192]{2,1,0:T(8,128)(2,1)} %all-gather.7.cloned.1.call-done), kind=kOutput, calls=%fused_computation.53 | convolution fusion | flops 4295229440 | bytes 36175872 | tf_op jit(solution)/shard_map/bpd,cd->bpc/dot_general | solution.py:80
  639.4 2.0 fusion.77
  641.5 1.8 fusion.107
  643.2 0.9 copy.53
  644.2 13.3 %fusion.93 = f32[2,2,128,8,64]{2,4,3,1,0:T(8,128)S(1)} fusion(f32[2,2,256,64,8]{2,3,4,1,0:T(8,128)} %fusion.107, bf16[2,256,2,128]{3,1,2,0:T(8,128)(2,1)} %copy-done.15, f32[2,2,8,64,256]{4,3,2,1,0:T(8,128)} %get-tuple-element.30, f32[2,2,8,64]{3,2,1,0:T(8,128)S(1)} %get-tuple-element.29), kind=kOutput, calls=%fused_computation.118 | convolution fusion | flops 137890048 | bytes 5513216 | tf_op jit(solution)/shard_map/bkgpj,bjkd->bpkgd/dot_general | solution.py:111
  657.6 1.7 slice_negate_fusion
  659.3 16.4 %fusion.78 = bf16[2,256,2,128]{3,1,2,0:T(8,128)(2,1)} fusion(bf16[2,64,2,8,128]{4,1,3,2,0:T(8,128)(2,1)} %bitcast.258, f32[2,2,256,64,8]{2,3,4,1,0:T(8,128)} %fusion.107, f32[2,2,8,64,256]{4,3,2,1,0:T(8,128)} %get-tuple-element.30, f32[2,2,8,64]{3,2,1,0:T(8,128)S(1)} %get-tuple-element.29), kind=kOutput, calls=%fused_computation.94 | convolution fusion | flops 138021120 | bytes 4988928 | tf_op jit(solution)/shard_map/bkgpj,bpkgd->bjkd/dot_general | solution.py:114
  676.0 13.0 %all-reduce.13.cloned.1.call-done = bf16[2,256,2,128]{3,2,0,1:T(2,128)(2,1)} async-done(((bf16[2,256,2,128]{3,2,0,1:T(2,128)(2,1)}), bf16[2,256,2,128]{3,2,0,1:T(2,128)(2,1)}) %all-reduce.13.cloned.1.call-update) | async-done | bytes 262160
  689.0 0.9 constant_dynamic-slice_fusion
  690.0 5.6 fusion.36
  695.6 20.5 %reduce-scatter.5.cloned.1.call-done = bf16[2,64,2,128]{3,1,2,0:T(8,128)(2,1)} async-done(((bf16[2,256,2,128]{3,1,2,0:T(8,128)(2,1)}), bf16[2,64,2,128]{3,1,2,0:T(8,128)(2,1)}) %reduce-scatter.5.cloned.1.call-update) | async-done | bytes 65552 | tf_op jit(solution)/shard_map/reduce_scatter | solution.py:121
  716.1 0.9 convert_multiply_fusion.4
  717.1 5.7 fusion.40
  722.8 19.2 %fusion.23 = bf16[2,64,8192]{2,1,0:T(8,128)(2,1)} fusion(f32[2,64,8192]{2,1,0:T(8,128)} %fusion.36, f32[2,64,8192]{2,1,0:T(8,128)} %fusion.40, bf16[1,8192,2048]{2,1,0:T(8,128)(2,1)} %param.16, f32[2,64,16,64]{3,1,2,0:T(8,128)} %get-tuple-element.11, f32[2,64,16,64]{3,1,2,0:T(8,128)} %get-tuple-element.10, f32[2,64,16,128]{3,1,2,0:T(8,128)S(1)} %bitcast.240, ...), kind=kOutput, calls=%fused_computation.15 | convolution fusion | flops 4299161600 | bytes 46170112 | tf_op jit(solution)/shard_map/bpc,dc->bpd/dot_general | solution.py:137
  742.1 86.3 %all-reduce.9.cloned.1.call-done = bf16[2,64,8192]{2,1,0:T(8,128)(2,1)} async-done(((bf16[2,64,8192]{2,1,0:T(8,128)(2,1)}), bf16[2,64,8192]{2,1,0:T(8,128)(2,1)}) %all-reduce.9.cloned.1.call-update) | async-done | bytes 2097168 | tf_op jit(solution)/shard_map/psum | solution.py:144
  828.4 2.2 convert_element_type.169
  830.6 0.9 fusion.32
  831.5 3.1 fusion.84
  (79 shorter events, 4.7 us)
Async XLA Ops:
  6.5 1.5 copy-start
  6.5 92.5 %all-gather.5.cloned.1.call-start = ((), (), s32[]{:S(2)}) async-start(), calls=%async_computation.6 | async-start | bytes 2621440 | tf_op jit(solution)/shard_map/all_gather | solution.py:58
  7.3 0.8 copy-start.16
  7.3 357.1 %all-gather.7.cloned.1.call-start = ((), (), s32[]{:S(2)}) async-start(), calls=%async_computation.7 | async-start | bytes 41943040 | tf_op jit(solution)/shard_map/all_gather | solution.py:158
  8.0 418.0 %all-reduce.11.cloned.1.call-start = ((), (), s32[]{:S(2)}) async-start(), calls=%async_computation.8 | async-start | bytes 524288
  8.5 60.0 %collective-permute-start = (bf16[2,64,2048]{2,1,0:T(8,128)(2,1)S(1)}, bf16[2,64,2048]{2,1,0:T(8,128)(2,1)S(1)}, u32[]{:S(2)}, u32[]{:S(2)}) collective-permute-start(bf16[2,64,2048]{2,1,0:T(8,128)(2,1)S(1)} %fusion.50), channel_id=1, source_target_pairs={{0,3},{1,0},{2,1},{3,2},{4,7},{5,4},{6,5},{7,6},{8,11},{9,8},{10,9... | collective-permute-start | bytes 1572872 | tf_op jit(solution)/shard_map/ppermute | solution.py:17
  60.9 6.4 copy-start.18
  60.9 7.7 copy-start.17
  67.2 33.9 %copy-start.13 = (f32[1,8192]{1,0:T(1,128)S(1)}, f32[1,8192]{1,0:T(1,128)}, u32[]{:S(2)}) copy-start(f32[1,8192]{1,0:T(1,128)} %param.15) | copy-start | bytes 98308
  68.5 13.4 %collective-permute-start.1 = (bf16[2,64,2048]{2,1,0:T(8,128)(2,1)S(1)}, bf16[2,64,2048]{2,1,0:T(8,128)(2,1)S(1)}, u32[]{:S(2)}, u32[]{:S(2)}) collective-permute-start(bf16[2,64,2048]{2,1,0:T(8,128)(2,1)S(1)} %collective-permute-done), channel_id=1, source_target_pairs={{0,3},{1,0},{2,1},{3,2},{4,7},{5,4},{6,5},{7,6},{8,11},{9,8},{10,9... | collective-permute-start | bytes 1572872 | tf_op jit(solution)/shard_map/ppermute | solution.py:17
  81.9 12.5 %collective-permute-start.2 = (bf16[2,64,2048]{2,1,0:T(8,128)(2,1)S(1)}, bf16[2,64,2048]{2,1,0:T(8,128)(2,1)S(1)}, u32[]{:S(2)}, u32[]{:S(2)}) collective-permute-start(bf16[2,64,2048]{2,1,0:T(8,128)(2,1)S(1)} %collective-permute-done.1), channel_id=1, source_target_pairs={{0,3},{1,0},{2,1},{3,2},{4,7},{5,4},{6,5},{7,6},{8,11},{9,8},{10,9... | collective-permute-start | bytes 1572872 | tf_op jit(solution)/shard_map/ppermute | solution.py:17
  101.1 16.5 %copy-start.2 = (bf16[1,2,64,8192]{3,2,1,0:T(8,128)(2,1)S(1)}, bf16[1,2,64,8192]{3,2,1,0:T(8,128)(2,1)}, u32[]{:S(2)}) copy-start(bf16[1,2,64,8192]{3,2,1,0:T(8,128)(2,1)} %all-gather.5.cloned.1.call-done) | copy-start | bytes 6291460
  101.2 16.5 %copy-start.8 = (bf16[256,8192]{1,0:T(8,128)(2,1)S(1)}, bf16[256,8192]{1,0:T(8,128)(2,1)}, u32[]{:S(2)}) copy-start(bf16[256,8192]{1,0:T(8,128)(2,1)} %copy.64) | copy-start | bytes 12582916
  117.6 30.4 %copy-start.15 = (bf16[2,256,2,128]{3,1,2,0:T(8,128)(2,1)}, bf16[2,256,2,128]{3,1,2,0:T(8,128)(2,1)S(1)}, u32[]{:S(2)}) copy-start(bf16[2,256,2,128]{3,1,2,0:T(8,128)(2,1)S(1)} %all_gather.16) | copy-start | bytes 786436
  131.4 251.3 %copy-start.10 = (bf16[2,256,2,128]{3,1,2,0:T(8,128)(2,1)}, bf16[2,256,2,128]{3,1,2,0:T(8,128)(2,1)S(1)}, u32[]{:S(2)}) copy-start(bf16[2,256,2,128]{3,1,2,0:T(8,128)(2,1)S(1)} %all_gather.17) | copy-start | bytes 786436
  148.0 232.8 %copy-start.14 = (bf16[2,64,16,128]{3,1,2,0:T(8,128)(2,1)}, bf16[2,64,16,128]{3,1,2,0:T(8,128)(2,1)S(1)}, u32[]{:S(2)}) copy-start(bf16[2,64,16,128]{3,1,2,0:T(8,128)(2,1)S(1)} %fusion.88) | copy-start | bytes 1572868
  364.4 16.6 %copy-start.12 = (bf16[2,2,8,64,256]{4,3,2,1,0:T(8,128)(2,1)S(1)}, bf16[2,2,8,64,256]{4,3,2,1,0:T(8,128)(2,1)}, u32[]{:S(2)}) copy-start(bf16[2,2,8,64,256]{4,3,2,1,0:T(8,128)(2,1)} %fusion.157) | copy-start | bytes 3145732
  382.7 70.3 %reduce-scatter.3.cloned.1.call-start = ((), (), s32[]{:S(2)}) async-start(), calls=%async_computation.2 | async-start | bytes 327680 | tf_op jit(solution)/shard_map/reduce_scatter | solution.py:121
  415.8 149.4 %all-reduce.7.cloned.1.call-start = ((), (), s32[]{:S(2)}) async-start(), calls=%async_computation.3 | async-start | bytes 4194304 | tf_op jit(solution)/shard_map/psum | solution.py:144
  478.9 210.1 %all-reduce.13.cloned.1.call-start = ((), (), s32[]{:S(2)}) async-start(), calls=%async_computation.9 | async-start | bytes 524288
  565.2 2.2 copy-start.7
  569.4 39.7 %copy-start.4 = (f32[2,64,8192]{2,1,0:T(8,128)}, f32[2,64,8192]{2,1,0:T(8,128)S(1)}, u32[]{:S(2)}) copy-start(f32[2,64,8192]{2,1,0:T(8,128)S(1)} %get-tuple-element.8) | copy-start | bytes 12582916
  569.4 49.4 %copy-start.5 = (f32[2,64,8192]{2,1,0:T(8,128)}, f32[2,64,8192]{2,1,0:T(8,128)S(1)}, u32[]{:S(2)}) copy-start(f32[2,64,8192]{2,1,0:T(8,128)S(1)} %get-tuple-element.22) | copy-start | bytes 12582916
  572.8 3.8 collective-permute-start.3
  576.6 14.0 %collective-permute-start.4 = (bf16[2,64,2048]{2,1,0:T(8,128)(2,1)S(1)}, bf16[2,64,2048]{2,1,0:T(8,128)(2,1)S(1)}, u32[]{:S(2)}, u32[]{:S(2)}) collective-permute-start(bf16[2,64,2048]{2,1,0:T(8,128)(2,1)S(1)} %collective-permute-done.3), channel_id=1, source_target_pairs={{0,3},{1,0},{2,1},{3,2},{4,7},{5,4},{6,5},{7,6},{8,11},{9,8},{10,9... | collective-permute-start | bytes 1572872 | tf_op jit(solution)/shard_map/ppermute | solution.py:17
  590.6 14.0 %collective-permute-start.5 = (bf16[2,64,2048]{2,1,0:T(8,128)(2,1)S(1)}, bf16[2,64,2048]{2,1,0:T(8,128)(2,1)S(1)}, u32[]{:S(2)}, u32[]{:S(2)}) collective-permute-start(bf16[2,64,2048]{2,1,0:T(8,128)(2,1)S(1)} %collective-permute-done.4), channel_id=1, source_target_pairs={{0,3},{1,0},{2,1},{3,2},{4,7},{5,4},{6,5},{7,6},{8,11},{9,8},{10,9... | collective-permute-start | bytes 1572872 | tf_op jit(solution)/shard_map/ppermute | solution.py:17
  604.6 14.2 %collective-permute-start.6 = (bf16[2,64,2048]{2,1,0:T(8,128)(2,1)S(1)}, bf16[2,64,2048]{2,1,0:T(8,128)(2,1)S(1)}, u32[]{:S(2)}, u32[]{:S(2)}) collective-permute-start(bf16[2,64,2048]{2,1,0:T(8,128)(2,1)S(1)} %collective-permute-done.5), channel_id=1, source_target_pairs={{0,3},{1,0},{2,1},{3,2},{4,7},{5,4},{6,5},{7,6},{8,11},{9,8},{10,9... | collective-permute-start | bytes 1572872 | tf_op jit(solution)/shard_map/ppermute | solution.py:17
  622.6 16.7 %copy-start.3 = (bf16[2,64,8192]{2,1,0:T(8,128)(2,1)}, bf16[2,64,8192]{2,1,0:T(8,128)(2,1)S(1)}, u32[]{:S(2)}) copy-start(bf16[2,64,8192]{2,1,0:T(8,128)(2,1)S(1)} %fusion.54) | copy-start | bytes 6291460
  622.6 18.9 %copy-start.11 = (bf16[2,256,2,128]{3,1,2,0:T(8,128)(2,1)S(1)}, bf16[2,256,2,128]{3,1,2,0:T(8,128)(2,1)}, u32[]{:S(2)}) copy-start(bf16[2,256,2,128]{3,1,2,0:T(8,128)(2,1)} %copy-done.10) | copy-start | bytes 786436
  644.1 72.0 %reduce-scatter.5.cloned.1.call-start = ((), (), s32[]{:S(2)}) async-start(), calls=%async_computation.4 | async-start | bytes 327680 | tf_op jit(solution)/shard_map/reduce_scatter | solution.py:121
  675.7 152.7 %all-reduce.9.cloned.1.call-start = ((), (), s32[]{:S(2)}) async-start(), calls=%async_computation.5 | async-start | bytes 4194304 | tf_op jit(solution)/shard_map/psum | solution.py:144
  742.1 89.4 %copy-start.9 = (f32[2,64,2048]{2,1,0:T(8,128)S(1)}, f32[2,64,2048]{2,1,0:T(8,128)}, u32[]{:S(2)}) copy-start(f32[2,64,2048]{2,1,0:T(8,128)} %get-tuple-element.7) | copy-start | bytes 3145732
  828.4 2.2 copy-start.6
  828.4 6.2 copy-start.1
Sparse Core Ops, SparseCore 0:
  8.9 50.2 all-gather.4
  61.0 303.3 all-gather.6
  382.8 43.2 all-reduce.10
  428.7 24.3 reduce-scatter.2
  479.1 86.1 all-reduce.6
  644.3 44.7 all-reduce.12
  691.8 24.3 reduce-scatter.4
  742.2 86.1 all-reduce.8
